TPU v7x, 32 devices: a whole 2x2x4 slice. The times are simulated.
32 devices in a mesh: view: 8 (over z, x), slab: 4 (over y, core).
Axes of the slice: x: 2, y: 2, z: 4, core: 2. Of those that a mesh axis runs over, the one named last changes fastest.
Arguments:
- volume: float32 [4, 128, 128], P('slab', 'view'), may hold values from 0 to 2
- tile_blocks: bfloat16 [8, 4, 192, 128, 128], P('view', 'slab'), may hold values from 0.0009994507 to 0.014953613
- pixel_tile: int32 [8, 4, 192], P('view', 'slab'), may hold values from 0 to 127, as said below
- ray_tile: int32 [8, 4, 192], P('view', 'slab'), may hold values from 0 to 127, as said below
- counts: int32 [8, 4], P('view', 'slab'), may hold values from 16 to 192, as said below
- subset_views: int32 [8, 4], P('view'), may hold values from 0 to 7, as said below
- sinogram: float32 [8, 128, 128], P('view', 'slab'), may hold values from 0 to 3
- weights: float32 [8, 128, 128], P('view', 'slab'), may hold values from 0.1 to 1
Outputs:
- updated: float32 [4, 128, 128], P('slab', 'view')
- denominators: float32 [4, 128, 128], P('slab', 'view')
Inputs may be any that keep to these rules, and one draw needn't show every extreme that they name: `counts`: for every group exactly one slab has 192 live slots; every count is at least 16. `pixel_tile`: slots k < 16 of group g name volume tiles g * 16 + k in every slab; slots at or past the count hold indices in range and are unused. `ray_tile`: slots at or past the count hold indices in range and are unused. `subset_views`: each group lists 4 distinct views in rising order.
All inputs are finite; a program needn't handle non-finite values.
Results may differ from a plain program's by a relative error of at most 0.00032.
Values may be sent and summed in bfloat16 or wider, within the bound.
No kernel may reach another device: no remote copies, remote signals or barrier semaphores. Data moves between devices by JAX's collectives and lax.ppermute only.
A program may use at most 64 MiB of HBM per device.

v0:
```python
import jax
import jax.numpy as jnp
from jax import lax
from jax.sharding import PartitionSpec as P

VG = 8
SUBSETS = 2


def make_ratio(totals, measured, weight, subset):
    ray_rows = jnp.arange(totals.shape[0], dtype=jnp.int32)
    view_of = ray_rows % VG
    in_subset = jnp.any(subset[None, :] == view_of[:, None], axis=1).astype(jnp.float32)
    denominator_rays = weight * totals[:, 1]
    residual_rays = in_subset[:, None] * weight * (measured - totals[:, 0])
    return jnp.stack([denominator_rays, residual_rays], axis=1).astype(jnp.bfloat16)


def on_device(volume, tile_blocks, pixel_tile, ray_tile, counts, subset_views, sinogram, weights):
    local_tiles = tile_blocks[0, 0]
    pixel_rows = pixel_tile[0, 0]
    ray_rows = ray_tile[0, 0]
    count_here = counts[0, 0]
    subset = subset_views[0]
    ray_total = sinogram.shape[1] * lax.axis_size("slab")
    voxel_total = volume.shape[1] * lax.axis_size("view")
    live_mask = (jnp.arange(local_tiles.shape[0], dtype=jnp.int32) < count_here).astype(jnp.float32)
    own_image = volume[0].astype(jnp.bfloat16)
    slab_image = lax.all_gather(own_image, "view", axis=0, tiled=True)
    picked = slab_image[pixel_rows]
    operand = jnp.stack([picked, jnp.ones_like(picked)], axis=1)
    products = jnp.einsum("krv,kcv->kcr", local_tiles, operand, preferred_element_type=jnp.float32)
    products = products * live_mask[:, None, None]
    partial_rays = jax.ops.segment_sum(products, ray_rows, num_segments=ray_total)
    measured, weight = (
        lax.all_gather(sinogram[0], "slab", axis=0, tiled=True),
        lax.all_gather(weights[0], "slab", axis=0, tiled=True),
    )
    totals = lax.psum(partial_rays, "slab")
    back_in = make_ratio(totals, measured, weight, subset)
    gathered = back_in[ray_rows]
    back_products = jnp.einsum(
        "krv,kcr->kcv", local_tiles, gathered, preferred_element_type=jnp.float32
    )
    back_products = back_products * live_mask[:, None, None]
    partial_voxels = jax.ops.segment_sum(back_products, pixel_rows, num_segments=voxel_total)
    voxel_share = lax.psum_scatter(partial_voxels, "view", scatter_dimension=0, tiled=True)
    denominators = voxel_share[:, 0, :]
    gradient = voxel_share[:, 1, :]
    updated = jnp.maximum(volume[0] + SUBSETS * gradient / denominators, 0.0)
    return (updated[None], denominators[None])


def solution(mesh):
    return jax.shard_map(
        on_device,
        mesh=mesh,
        in_specs=(
            P("slab", "view", None),
            P("view", "slab", None, None, None),
            P("view", "slab", None),
            P("view", "slab", None),
            P("view", "slab"),
            P("view", None),
            P("view", "slab", None),
            P("view", "slab", None),
        ),
        out_specs=(P("slab", "view", None), P("slab", "view", None)),
        check_vma=False,
    )
```

profile of v0, /device:TPU:0, one launch (start us, length us, event | category | flops | bytes accessed | tf_op | source)
XLA Modules:
  0.0 182.9 jit_solution(6079675270705240020)
XLA Ops:
  7.9 0.7 convert_element_type.21
  8.6 32.4 %all-gather.1 = bf16[1,128,128]{2,1,0:T(8,128)(2,1)S(1)} all-gather(bf16[1,16,128]{2,1,0:T(8,128)(2,1)S(1)} %convert_element_type.21), channel_id=3, replica_groups=mesh['view'=8,'slab'=4] {'view'}, dimensions={1}, use_global_device_ids=true | all-gather | bytes 36864 | tf_op jit(solution)/shard_map/all_gather | solution.py:29
  41.0 0.7 compare_select_fusion.1
  41.7 0.8 gather_fusion
  42.5 0.1 copy.19
  42.6 6.1 %fusion.4 = f32[192,2,128]{2,1,0:T(2,128)S(1)} fusion(bf16[1,1,192,128,128]{4,3,2,1,0:T(8,128)(2,1)} %param.9, f32[192]{0:T(256)S(1)} %compare_convert_fusion, bf16[192,1,128]{2,1,0:T(2,128)(2,1)S(1)} %copy.19), kind=kOutput, calls=%fused_computation.8 | convolution fusion | flops 12632064 | bytes 6537984 | tf_op jit(solution)/shard_map/krv,kcv->kcr/dot_general | solution.py:32
  48.8 7.2 %scatter_fusion = f32[128,2,128]{2,1,0:T(2,128)S(1)} fusion(f32[128,2,128]{2,1,0:T(2,128)S(1)} %broadcast.74.clone, s32[192]{0:T(256)S(1)} %bitcast.68, f32[192,2,128]{2,1,0:T(2,128)S(1)} %fusion.4), kind=kCustom, calls=%fused_computation.2 | custom fusion | flops 49152 | bytes 590592 | tf_op jit(solution)/shard_map/scatter-add | solution.py:34
  56.0 0.6 copy-done.1
  56.6 0.0 all-reduce.7.cloned.1.call-start
  56.7 0.1 compare_reduce_fusion
  56.8 5.2 %all-gather = f32[1,128,128]{2,1,0:T(8,128)S(1)} all-gather(f32[1,32,128]{2,1,0:T(8,128)S(1)} %copy-done.4), channel_id=2, replica_groups=mesh['view'=8,'slab'=4] {'slab'}, dimensions={1}, use_global_device_ids=true | all-gather | bytes 81920 | tf_op jit(solution)/shard_map/all_gather | solution.py:37
  62.1 5.2 %all-gather.2 = f32[1,128,128]{2,1,0:T(8,128)S(1)} all-gather(f32[1,32,128]{2,1,0:T(8,128)S(1)} %copy-done.5), channel_id=4, replica_groups=mesh['view'=8,'slab'=4] {'slab'}, dimensions={1}, use_global_device_ids=true | all-gather | bytes 81920 | tf_op jit(solution)/shard_map/all_gather | solution.py:36
  67.3 22.2 %all-reduce.5.cloned.1.call-done = f32[128,2,128]{2,1,0:T(2,128)} async-done(((f32[128,2,128]{2,1,0:T(2,128)}), f32[128,2,128]{2,1,0:T(2,128)}) %all-reduce.5.cloned.1.call-update) | async-done | bytes 131088 | tf_op jit(solution)/shard_map/psum | solution.py:39
  89.5 1.1 fusion.19
  90.5 0.1 fusion.14
  90.7 0.1 copy.21
  90.7 0.8 gather_fusion.1
  91.6 4.5 %fusion.7 = f32[192,2,128]{2,1,0:T(2,128)S(1)} fusion(bf16[192,2,128]{2,1,0:T(2,128)(2,1)S(1)} %gather_fusion.1, bf16[1,1,192,128,128]{4,3,2,1,0:T(8,128)(2,1)} %param.9, f32[192]{0:T(256)S(1)} %compare_convert_fusion), kind=kOutput, calls=%fused_computation.9 | convolution fusion | flops 12632064 | bytes 6587136 | tf_op jit(solution)/shard_map/krv,kcr->kcv/dot_general | solution.py:42
  96.2 7.1 %scatter_fusion.1 = f32[128,2,128]{2,1,0:T(2,128)S(1)} fusion(f32[128,2,128]{2,1,0:T(2,128)S(1)} %broadcast.74, s32[192]{0:T(256)S(1)} %bitcast.69, f32[192,2,128]{2,1,0:T(2,128)S(1)} %fusion.7), kind=kCustom, calls=%fused_computation.3 | custom fusion | flops 49152 | bytes 590592 | tf_op jit(solution)/shard_map/scatter-add | solution.py:46
  103.3 0.6 copy-done
  104.0 0.6 dynamic-slice
  105.2 69.4 %all-reduce.7.cloned.1.call-done = f32[128,2,128]{2,1,0:T(2,128)} async-done(((f32[128,2,128]{2,1,0:T(2,128)}), f32[128,2,128]{2,1,0:T(2,128)}) %all-reduce.7.cloned.1.call-update) | async-done | bytes 131088
  174.6 0.8 constant_dynamic-slice_fusion
  175.5 0.6 fusion.17
  (30 shorter events, 0.2 us)
Async XLA Ops:
  7.2 41.6 %copy-start.6 = (s32[1,1,192]{2,1,0:T(1,128)S(1)}, s32[1,1,192]{2,1,0:T(1,128)}, u32[]{:S(2)}) copy-start(s32[1,1,192]{2,1,0:T(1,128)} %param.11) | copy-start | bytes 2308
  7.2 49.5 %copy-start.8 = (s32[1,4]{1,0:T(1,128)S(1)}, s32[1,4]{1,0:T(1,128)}, u32[]{:S(2)}) copy-start(s32[1,4]{1,0:T(1,128)} %param.13) | copy-start | bytes 52
  7.2 49.6 %copy-start.4 = (f32[1,32,128]{2,1,0:T(8,128)S(1)}, f32[1,32,128]{2,1,0:T(8,128)}, u32[]{:S(2)}) copy-start(f32[1,32,128]{2,1,0:T(8,128)} %param.15) | copy-start | bytes 49156
  7.2 54.9 %copy-start.5 = (f32[1,32,128]{2,1,0:T(8,128)S(1)}, f32[1,32,128]{2,1,0:T(8,128)}, u32[]{:S(2)}) copy-start(f32[1,32,128]{2,1,0:T(8,128)} %param.14) | copy-start | bytes 49156
  7.2 82.2 %all-reduce.5.cloned.1.call-start = ((), (), s32[]{:S(2)}) async-start(), calls=%async_computation | async-start | bytes 262144 | tf_op jit(solution)/shard_map/psum | solution.py:39
  42.6 53.6 %copy-start.7 = (s32[1,1,192]{2,1,0:T(1,128)S(1)}, s32[1,1,192]{2,1,0:T(1,128)}, u32[]{:S(2)}) copy-start(s32[1,1,192]{2,1,0:T(1,128)} %param.10) | copy-start | bytes 2308
  48.7 55.3 %copy-start.9 = (u32[32]{0:T(128)S(1)}, u32[32]{0:T(128)}, u32[]{:S(2)}) copy-start(u32[32]{0:T(128)} %constant.40) | copy-start | bytes 388
  48.7 126.7 %copy-start.2 = (f32[1,16,128]{2,1,0:T(8,128)S(1)}, f32[1,16,128]{2,1,0:T(8,128)}, u32[]{:S(2)}) copy-start(f32[1,16,128]{2,1,0:T(8,128)} %param.8) | copy-start | bytes 24580
  55.9 0.7 copy-start.1
  56.6 118.0 %all-reduce.7.cloned.1.call-start = ((), (), s32[]{:S(2)}) async-start(), calls=%async_computation.1 | async-start | bytes 262144
  103.3 0.7 copy-start
  175.4 0.6 copy-start.3
Sparse Core Ops, SparseCore 0:
  56.7 32.6 all-reduce.4
  104.1 70.4 all-reduce.6
where the time goes:
time: 183 us
  waiting for transfers between devices  91.6 us (50%)
  blocking collectives  42.9 us (23%)
  other arithmetic  16.5 us (9%)
  between operations  15.5 us (8%)
  matrix products  10.7 us (6%)
  local copies, waits for them, and re-layouts  5.65 us (3%)
    unnamed x3, waiting for transfers between devices  69.4 us
    all_gather x1, blocking collectives, on_device(): slab_image = lax.all_gather(own_image, 'view', axis=0, tiled=True)  32.4 us
    psum x1, waiting for transfers between devices, on_device(): totals = lax.psum(partial_rays, 'slab')  22.2 us
    scatter-add x1, other arithmetic, on_device(): jax.ops.segment_sum(products, ray_rows, num_segments=ray_total)  7.15 us
    scatter-add x1, other arithmetic, on_device(): jax.ops.segment_sum(back_products, pixel_rows, num_segments=voxel_total)  7.15 us
    dot_general x1, matrix products, on_device(): jnp.einsum('krv,kcv->kcr', local_tiles, operand, preferred_element_type=j...  6.14 us
    all_gather x1, blocking collectives, on_device(): lax.all_gather(sinogram[0], 'slab', axis=0, tiled=True)  5.24 us
    all_gather x1, blocking collectives, on_device(): lax.all_gather(weights[0], 'slab', axis=0, tiled=True)  5.24 us
  transfers between devices with their start and end apart: 2, of which 2 were waited for; matrix products, arithmetic and copies ran while one was open for 0% of the time, Pallas kernels for 0%

commit v1 on v0

--- a/solution.py
+++ b/solution.py
@@ -36,7 +36,7 @@
         lax.all_gather(sinogram[0], "slab", axis=0, tiled=True),
         lax.all_gather(weights[0], "slab", axis=0, tiled=True),
     )
-    totals = lax.psum(partial_rays, "slab")
+    totals = jnp.sum(lax.all_gather(partial_rays, "slab"), axis=0)
     back_in = make_ratio(totals, measured, weight, subset)
     gathered = back_in[ray_rows]
     back_products = jnp.einsum(

time: 183 us -> 168 us (0.918)
  waiting for transfers between devices: 91.6 us -> 69.6 us
  blocking collectives: 42.9 us -> 50.1 us
    psum x1 -> x0, waiting for transfers between devices: 22.2 us -> none  [on_device(): totals = lax.psum(partial_rays, 'slab')]
    all_gather x0 -> x1, blocking collectives: none -> 7.2 us  [on_device(): totals = jnp.sum(lax.all_gather(partial_rays, 'slab'), axis=0)]
    unnamed x3 -> x2, waiting for transfers between devices: 69.4 us -> 69.6 us
  transfers between devices with their start and end apart: 2 -> 1, of which waited for: 2 -> 1; matrix products, arithmetic and copies ran while one was open for 0% -> 0% of each run, Pallas kernels for 0% -> 0%
where the time goes in v1:
time: 168 us
  waiting for transfers between devices  69.6 us (41%)
  blocking collectives  50.1 us (30%)
  other arithmetic  17.6 us (10%)
  between operations  15.5 us (9%)
  matrix products  10.6 us (6%)
  local copies, waits for them, and re-layouts  4.07 us (2%)
    unnamed x2, waiting for transfers between devices  69.6 us
    all_gather x1, blocking collectives, on_device(): slab_image = lax.all_gather(own_image, 'view', axis=0, tiled=True)  32.4 us
    all_gather x1, blocking collectives, on_device(): totals = jnp.sum(lax.all_gather(partial_rays, 'slab'), axis=0)  7.2 us
    scatter-add x1, other arithmetic, on_device(): jax.ops.segment_sum(products, ray_rows, num_segments=ray_total)  7.15 us
    scatter-add x1, other arithmetic, on_device(): jax.ops.segment_sum(back_products, pixel_rows, num_segments=voxel_total)  7.15 us
    dot_general x1, matrix products, on_device(): jnp.einsum('krv,kcv->kcr', local_tiles, operand, preferred_element_type=j...  6.11 us
    all_gather x1, blocking collectives, on_device(): lax.all_gather(weights[0], 'slab', axis=0, tiled=True)  5.24 us
    all_gather x1, blocking collectives, on_device(): lax.all_gather(sinogram[0], 'slab', axis=0, tiled=True)  5.22 us
  transfers between devices with their start and end apart: 1, of which 1 were waited for; matrix products, arithmetic and copies ran while one was open for 0% of the time, Pallas kernels for 0%

profile of v1, /device:TPU:0, one launch (start us, length us, event | category | flops | bytes accessed | tf_op | source)
XLA Modules:
  0.0 167.5 jit_solution(2142970702210388221)
XLA Ops:
  7.9 0.7 convert_element_type.21
  8.6 32.4 %all-gather.1 = bf16[1,128,128]{2,1,0:T(8,128)(2,1)S(1)} all-gather(bf16[1,16,128]{2,1,0:T(8,128)(2,1)S(1)} %convert_element_type.21), channel_id=3, replica_groups=mesh['view'=8,'slab'=4] {'view'}, dimensions={1}, use_global_device_ids=true | all-gather | bytes 36864 | tf_op jit(solution)/shard_map/all_gather | solution.py:29
  41.0 0.7 compare_select_fusion.1
  41.7 0.8 gather_fusion
  42.5 0.1 copy.26
  42.6 0.7 compare_select_fusion
  43.3 6.1 %fusion.4 = f32[192,2,128]{2,1,0:T(2,128)S(1)} fusion(bf16[1,1,192,128,128]{4,3,2,1,0:T(8,128)(2,1)} %param.9, f32[192]{0:T(256)S(1)} %compare_convert_fusion, bf16[192,1,128]{2,1,0:T(2,128)(2,1)S(1)} %copy.26), kind=kOutput, calls=%fused_computation.8 | convolution fusion | flops 12632064 | bytes 6537984 | tf_op jit(solution)/shard_map/krv,kcv->kcr/dot_general | solution.py:32
  49.5 7.2 %scatter_fusion = f32[128,2,128]{2,1,0:T(2,128)S(1)} fusion(f32[128,2,128]{2,1,0:T(2,128)S(1)} %broadcast.74.clone, s32[192]{0:T(256)S(1)} %bitcast.70, f32[192,2,128]{2,1,0:T(2,128)S(1)} %fusion.4), kind=kCustom, calls=%fused_computation.2 | custom fusion | flops 49152 | bytes 590592 | tf_op jit(solution)/shard_map/scatter-add | solution.py:34
  56.6 7.2 %all-gather.2 = f32[512,2,128]{2,1,0:T(2,128)S(1)} all-gather(f32[128,2,128]{2,1,0:T(2,128)S(1)} %scatter_fusion), channel_id=4, replica_groups=mesh['view'=8,'slab'=4] {'slab'}, dimensions={0}, use_global_device_ids=true | all-gather | bytes 655360 | tf_op jit(solution)/shard_map/all_gather | solution.py:39
  63.8 0.3 reduce_sum.9
  64.1 0.1 fusion.19
  64.2 5.2 %all-gather = f32[1,128,128]{2,1,0:T(8,128)S(1)} all-gather(f32[1,32,128]{2,1,0:T(8,128)S(1)} %copy-done.3), channel_id=2, replica_groups=mesh['view'=8,'slab'=4] {'slab'}, dimensions={1}, use_global_device_ids=true | all-gather | bytes 81920 | tf_op jit(solution)/shard_map/all_gather | solution.py:37
  69.5 5.2 %all-gather.3 = f32[1,128,128]{2,1,0:T(8,128)S(1)} all-gather(f32[1,32,128]{2,1,0:T(8,128)S(1)} %copy-done.4), channel_id=5, replica_groups=mesh['view'=8,'slab'=4] {'slab'}, dimensions={1}, use_global_device_ids=true | all-gather | bytes 81920 | tf_op jit(solution)/shard_map/all_gather | solution.py:36
  74.7 0.1 compare_reduce_fusion
  74.8 0.1 fusion.14
  75.0 0.2 pad_maximum_fusion
  75.2 0.8 gather_fusion.1
  76.0 4.5 %fusion.7 = f32[192,2,128]{2,1,0:T(2,128)S(1)} fusion(bf16[192,2,128]{2,1,0:T(2,128)(2,1)S(1)} %gather_fusion.1, bf16[1,1,192,128,128]{4,3,2,1,0:T(8,128)(2,1)} %param.9, f32[192]{0:T(256)S(1)} %compare_convert_fusion), kind=kOutput, calls=%fused_computation.9 | convolution fusion | flops 12632064 | bytes 6587136 | tf_op jit(solution)/shard_map/krv,kcr->kcv/dot_general | solution.py:42
  80.6 7.1 %scatter_fusion.1 = f32[128,2,128]{2,1,0:T(2,128)S(1)} fusion(f32[128,2,128]{2,1,0:T(2,128)S(1)} %broadcast.74, s32[192]{0:T(256)S(1)} %bitcast.71, f32[192,2,128]{2,1,0:T(2,128)S(1)} %fusion.7), kind=kCustom, calls=%fused_computation.3 | custom fusion | flops 49152 | bytes 590592 | tf_op jit(solution)/shard_map/scatter-add | solution.py:46
  87.8 0.6 copy-done
  88.4 0.6 dynamic-slice
  89.7 69.6 %all-reduce.4.cloned.1.call-done = f32[128,2,128]{2,1,0:T(2,128)} async-done(((f32[128,2,128]{2,1,0:T(2,128)}), f32[128,2,128]{2,1,0:T(2,128)}) %all-reduce.4.cloned.1.call-update) | async-done | bytes 131088
  159.2 0.8 constant_dynamic-slice_fusion
  160.1 0.6 fusion.17
  (28 shorter events, 0.3 us)
Async XLA Ops:
  7.2 42.3 %copy-start.5 = (s32[1,1,192]{2,1,0:T(1,128)S(1)}, s32[1,1,192]{2,1,0:T(1,128)}, u32[]{:S(2)}) copy-start(s32[1,1,192]{2,1,0:T(1,128)} %param.11) | copy-start | bytes 2308
  7.2 57.0 %copy-start.3 = (f32[1,32,128]{2,1,0:T(8,128)S(1)}, f32[1,32,128]{2,1,0:T(8,128)}, u32[]{:S(2)}) copy-start(f32[1,32,128]{2,1,0:T(8,128)} %param.15) | copy-start | bytes 49156
  7.2 62.3 %copy-start.4 = (f32[1,32,128]{2,1,0:T(8,128)S(1)}, f32[1,32,128]{2,1,0:T(8,128)}, u32[]{:S(2)}) copy-start(f32[1,32,128]{2,1,0:T(8,128)} %param.14) | copy-start | bytes 49156
  7.2 67.5 %copy-start.7 = (s32[1,4]{1,0:T(1,128)S(1)}, s32[1,4]{1,0:T(1,128)}, u32[]{:S(2)}) copy-start(s32[1,4]{1,0:T(1,128)} %param.13) | copy-start | bytes 52
  7.2 152.0 %all-reduce.4.cloned.1.call-start = ((), (), s32[]{:S(2)}) async-start(), calls=%async_computation | async-start | bytes 262144
  49.4 31.2 %copy-start.6 = (s32[1,1,192]{2,1,0:T(1,128)S(1)}, s32[1,1,192]{2,1,0:T(1,128)}, u32[]{:S(2)}) copy-start(s32[1,1,192]{2,1,0:T(1,128)} %param.10) | copy-start | bytes 2308
  49.4 39.0 %copy-start.8 = (u32[32]{0:T(128)S(1)}, u32[32]{0:T(128)}, u32[]{:S(2)}) copy-start(u32[32]{0:T(128)} %constant.41) | copy-start | bytes 388
  49.4 110.7 %copy-start.1 = (f32[1,16,128]{2,1,0:T(8,128)S(1)}, f32[1,16,128]{2,1,0:T(8,128)}, u32[]{:S(2)}) copy-start(f32[1,16,128]{2,1,0:T(8,128)} %param.8) | copy-start | bytes 24580
  87.7 0.7 copy-start
  160.1 0.6 copy-start.2
Sparse Core Ops, SparseCore 0:
  88.5 70.6 all-reduce.3
